TPU v7x, 32 devices: a whole 2x2x4 slice. The times are simulated.
32 devices in a mesh: rows: 8 (over y, x, core), sub: 4 (over z).
Axes of the slice: x: 2, y: 2, z: 4, core: 2. Of those that a mesh axis runs over, the one named last changes fastest.
Arguments:
- old_basis: bfloat16 [32, 524288], P(None, ('rows', 'sub')), may hold values from -1 to 1
- snapshots: bfloat16 [512, 524288], P(None, ('rows', 'sub')), may hold values from -16 to 16
- gap_flags: int32 [512, 4096], P(None, ('rows', 'sub')), may hold values from 0 to 1, as said below
- sketch_seed: int32 [512, 64], replicated, may hold values from -1 to 1
Outputs:
- new_basis: float32 [32, 524288], P(None, ('rows', 'sub'))
- coefficients: float32 [32, 512], replicated
Inputs may be any that keep to these rules, and one draw needn't show every extreme that they name: `gap_flags`: 1 marks a block of 128 velocity rows measured in that snapshot, 0 a gap; every snapshot has measured blocks and gaps.
All inputs are finite; a program needn't handle non-finite values.
Results may differ from a plain program's by a relative error of at most 0.00135.
The roundings to bfloat16 on the way count: a program that leaves them out, or rounds other values in their place, can miss the bound.
Values may be sent and summed in bfloat16 or wider, within the bound.
No kernel may reach another device: no remote copies, remote signals or barrier semaphores. Data moves between devices by JAX's collectives and lax.ppermute only.
A program may use at most 192 MiB of HBM per device.

v0:
```python
import math
import jax
import jax.numpy as jnp
from jax import lax
from jax.sharding import PartitionSpec as P

POWER = 2
damping = 0.005
highest = lax.Precision.HIGHEST


def cholesky_last(system):
    extent = system.shape[0]
    factor = jnp.zeros_like(system)
    for column in range(extent):
        partial_sum = jnp.sum(factor * factor[column : column + 1], axis=1)
        remain = system[:, column] - partial_sum
        diagonal_root = jnp.sqrt(remain[column])
        lower_part = (jnp.arange(extent) >= column).reshape((extent,) + (1,) * (system.ndim - 2))
        factor = factor.at[:, column].set(jnp.where(lower_part, remain / diagonal_root, 0.0))
    return factor


def lower_solve(factor, target):
    extent = factor.shape[0]
    result = jnp.zeros_like(target)
    for column in range(extent):
        current = (target[column] - jnp.sum(factor[column] * result, axis=0)) / factor[
            column, column
        ]
        result = result.at[column].set(current)
    return result


def upper_solve(factor, target):
    extent = factor.shape[0]
    result = jnp.zeros_like(target)
    for column in reversed(range(extent)):
        current = (target[column] - jnp.sum(factor[:, column] * result, axis=0)) / factor[
            column, column
        ]
        result = result.at[column].set(current)
    return result


def solve_normal(grams, right, modes, rows_all):
    snapshot_count = grams.shape[0]
    identity = jnp.eye(modes, dtype=jnp.float32)[:, :, None]
    system = grams.T.reshape(modes, modes, snapshot_count) + damping * rows_all * identity
    factor = cholesky_last(system)
    return upper_solve(factor, lower_solve(factor, right.T))


def inverse_factor(products):
    extent = products.shape[0]
    factor = cholesky_last(products[:, :, None])
    return lower_solve(factor, jnp.eye(extent, dtype=jnp.float32))


def mask_blocks(samples, flag_blocks):
    snapshot_count, blocks_dev = flag_blocks.shape
    weights = flag_blocks.astype(samples.dtype)[:, :, None]
    return (samples.reshape(snapshot_count, blocks_dev, -1) * weights).reshape(snapshot_count, -1)


def refill(samples, flag_blocks, recon_low):
    snapshot_count, blocks_dev = flag_blocks.shape
    observed = (flag_blocks > 0)[:, :, None]
    combined = jnp.where(
        observed,
        samples.reshape(snapshot_count, blocks_dev, -1),
        recon_low.reshape(snapshot_count, blocks_dev, -1),
    )
    return combined.reshape(snapshot_count, -1)


def contract_rows(former, latter):
    return lax.dot_general(
        former, latter, (((1,), (1,)), ((), ())), preferred_element_type=jnp.float32
    )


def contract_first(former, latter):
    return lax.dot_general(
        former, latter, (((0,), (0,)), ((), ())), preferred_element_type=jnp.float32
    )


def per_device(old_basis, snapshots, gap_flags, sketch_seed):
    modes = old_basis.shape[0]
    rows_all = old_basis.shape[1] * lax.axis_size(("rows", "sub"))
    blocks_dev = gap_flags.shape[1]
    masked = mask_blocks(snapshots, gap_flags)
    right = contract_rows(masked, old_basis)
    pieces = old_basis.reshape(modes, blocks_dev, -1)
    block_grams = jnp.einsum("kbi,lbi->bkl", pieces, pieces, preferred_element_type=jnp.float32)
    block_rows = block_grams.reshape(blocks_dev, modes * modes)
    grams = jnp.dot(gap_flags.astype(jnp.float32), block_rows, precision=highest)
    mixer = sketch_seed.astype(jnp.bfloat16)
    gram_total, right_total = lax.psum((grams, right), ("rows", "sub"))
    coefficients = solve_normal(gram_total, right_total, modes, rows_all)
    recon_low = contract_first(coefficients.astype(jnp.bfloat16), old_basis).astype(jnp.bfloat16)
    filled = refill(snapshots, gap_flags, recon_low)
    sketch = contract_first(mixer, filled)
    inverse = None
    for sweep_index in range(POWER + 1):
        if sweep_index > 0:
            sketch = contract_first(mixer, filled)
        local_gram = lax.dot_general(
            sketch,
            sketch,
            (((1,), (1,)), ((), ())),
            precision=highest,
            preferred_element_type=jnp.float32,
        )
        products = lax.psum(local_gram, ("rows", "sub"))
        inverse = inverse_factor(products)
        if sweep_index < POWER:
            ortho_rows = jnp.dot(inverse, sketch, precision=highest).astype(jnp.bfloat16)
            mixer_share = lax.psum_scatter(
                contract_rows(filled, ortho_rows), ("rows", "sub"), scatter_dimension=0, tiled=True
            ).astype(jnp.bfloat16)
            mixer = lax.all_gather(mixer_share, ("rows", "sub"), axis=0, tiled=True)
    root_rows = math.sqrt(rows_all)
    new_basis = jnp.dot(inverse[:modes], sketch, precision=highest) * root_rows
    return (new_basis, coefficients)


def solution(mesh):
    in_specs = (P(None, ("rows", "sub")), P(None, ("rows", "sub")), P(None, ("rows", "sub")), P())
    out_specs = (P(None, ("rows", "sub")), P())
    return jax.shard_map(
        per_device, mesh=mesh, in_specs=in_specs, out_specs=out_specs, check_vma=False
    )
```

profile of v0, /device:TPU:0, one launch (start us, length us, event | category | flops | bytes accessed | tf_op | source)
XLA Modules:
  0.0 1549.7 jit_solution(17264317991794373059)
XLA Ops:
  9.1 2.1 copy.518
  11.2 2.8 fusion.6
  14.1 2.5 copy.519
  16.6 13.0 mul.4308
  29.6 24.4 %fusion.2 = f32[32,512]{1,0:T(8,128)} fusion(bf16[32,16384]{1,0:T(8,128)(2,1)S(1)} %copy-done, bf16[512,16384]{1,0:T(8,128)(2,1)} %param.965, bf16[64,8,128,128]{3,2,1,0:T(8,128)(2,1)} %bitcast.3922), kind=kOutput, calls=%fused_computation.40 | convolution fusion | flops 545259520 | bytes 34668544 | tf_op jit(solution)/shard_map/dot_general | solution.py:78
  54.7 137.0 %all-reduce.12.cloned.1.call-done = (f32[32,32,512]{2,0,1:T(8,128)}, f32[32,512]{1,0:T(8,128)}) async-done(((f32[32,32,512]{2,0,1:T(8,128)}, f32[32,512]{1,0:T(8,128)}), (f32[32,32,512]{2,0,1:T(8,128)}, f32[32,512]{1,0:T(8,128)})) %all-reduce.12.cloned.1.call-update) | async-done | bytes 2162704 | tf_op jit(solution)/shard_map/psum | solution.py:100
  191.7 1.8 broadcast_add_fusion
  291.6 12.0 broadcast_in_dim.635
  303.5 15.2 bitcast_select_fusion
  318.8 8.8 fusion.224
  327.6 1.9 copy-done.5
  329.5 3.4 convolution_bitcast_fusion.2
  332.9 39.6 %psum.37 = f32[64,64,1]{1,0,2:T(8,128)S(1)} all-reduce(f32[64,64,1]{1,0,2:T(8,128)S(1)} %convolution_bitcast_fusion.2), channel_id=1, replica_groups=mesh['rows'=8,'sub'=4] {'rows','sub'}, use_global_device_ids=true, to_apply=%region_97.98 | all-reduce | flops 4096 | bytes 32768 | tf_op jit(solution)/shard_map/psum | solution.py:116
  498.8 1.4 fusion.505
  500.2 1.4 fusion.504
  510.2 1.4 fusion.497
  511.7 1.4 fusion.496
  516.1 1.4 fusion.493
  530.4 1.4 fusion.483
  537.6 1.4 fusion.478
  566.0 1.4 fusion.458
  578.8 1.4 fusion.449
  581.6 6.0 convolution_convert_fusion.2
  587.6 8.8 fusion.526
  596.5 133.4 %reduce-scatter.3.cloned.1.call-done = f32[16,64]{1,0:T(8,128)} async-done(((f32[512,64]{1,0:T(8,128)}), f32[16,64]{1,0:T(8,128)}) %reduce-scatter.3.cloned.1.call-update) | async-done | bytes 4112 | tf_op jit(solution)/shard_map/reduce_scatter | solution.py:120
  730.6 64.8 %all_gather.6 = bf16[512,64]{1,0:T(8,128)(2,1)S(1)} all-gather(bf16[16,64]{1,0:T(8,128)(2,1)S(1)} %convert_element_type.415), channel_id=1, replica_groups=mesh['rows'=8,'sub'=4] {'rows','sub'}, dimensions={0}, use_global_device_ids=true | all-gather | bytes 67584 | tf_op jit(solution)/shard_map/all_gather | solution.py:123
  795.3 8.9 fusion.527
  804.2 1.9 copy-done.4
  806.2 3.4 convolution_bitcast_fusion.1
  809.6 39.9 %psum.38 = f32[64,64,1]{1,0,2:T(8,128)S(1)} all-reduce(f32[64,64,1]{1,0,2:T(8,128)S(1)} %convolution_bitcast_fusion.1), channel_id=1, replica_groups=mesh['rows'=8,'sub'=4] {'rows','sub'}, use_global_device_ids=true, to_apply=%region_226.227 | all-reduce | flops 4096 | bytes 32768 | tf_op jit(solution)/shard_map/psum | solution.py:116
  970.7 1.9 subtract_divide_fusion.3
  972.7 1.4 fusion.447
  974.2 1.4 fusion.446
  979.9 1.4 fusion.442
  981.4 1.4 fusion.441
  991.3 1.4 fusion.434
  997.2 1.4 fusion.430
  1011.5 1.4 fusion.420
  1018.7 1.4 fusion.415
  1047.1 1.4 fusion.395
  1059.9 1.4 fusion.386
  1062.7 6.0 convolution_convert_fusion.1
  1068.7 8.8 fusion.528
  1077.5 133.0 %reduce-scatter.5.cloned.1.call-done = f32[16,64]{1,0:T(8,128)} async-done(((f32[512,64]{1,0:T(8,128)}), f32[16,64]{1,0:T(8,128)}) %reduce-scatter.5.cloned.1.call-update) | async-done | bytes 4112 | tf_op jit(solution)/shard_map/reduce_scatter | solution.py:120
  1211.2 64.8 %all_gather.7 = bf16[512,64]{1,0:T(8,128)(2,1)S(1)} all-gather(bf16[16,64]{1,0:T(8,128)(2,1)S(1)} %convert_element_type.417), channel_id=1, replica_groups=mesh['rows'=8,'sub'=4] {'rows','sub'}, dimensions={0}, use_global_device_ids=true | all-gather | bytes 67584 | tf_op jit(solution)/shard_map/all_gather | solution.py:123
  1276.0 8.9 fusion.529
  1284.9 1.9 copy-done.3
  1286.8 3.4 convolution_bitcast_fusion
  1290.2 39.9 %psum.39 = f32[64,64,1]{1,0,2:T(8,128)S(1)} all-reduce(f32[64,64,1]{1,0,2:T(8,128)S(1)} %convolution_bitcast_fusion), channel_id=1, replica_groups=mesh['rows'=8,'sub'=4] {'rows','sub'}, use_global_device_ids=true, to_apply=%region_355.356 | all-reduce | flops 4096 | bytes 32768 | tf_op jit(solution)/shard_map/psum | solution.py:116
  1450.6 1.9 subtract_divide_fusion.2
  1452.6 1.4 fusion.384
  1455.5 1.4 fusion.382
  1462.7 1.4 fusion.377
  1467.0 1.4 fusion.374
  1468.5 1.4 fusion.373
  1471.4 1.4 fusion.371
  1482.8 1.4 fusion.363
  1484.2 1.4 fusion.362
  1498.5 1.4 fusion.352
  1508.6 1.4 fusion.345
  1520.1 1.4 fusion.337
  1530.0 1.4 fusion.330
  1532.9 1.4 fusion.328
  1537.1 5.7 convolution_multiply_fusion
  (2302 shorter events, 543.1 us)
Async XLA Ops:
  7.2 1.3 copy-start
  7.2 184.5 %all-reduce.12.cloned.1.call-start = ((), (), s32[]{:S(2)}) async-start(), calls=%async_computation.4 | async-start | bytes 4325376 | tf_op jit(solution)/shard_map/psum | solution.py:100
  9.1 2.1 copy-start.8
  54.0 675.8 %reduce-scatter.3.cloned.1.call-start = ((), (), s32[]{:S(2)}) async-start(), calls=%async_computation.2 | async-start | bytes 270336 | tf_op jit(solution)/shard_map/reduce_scatter | solution.py:120
  54.7 443.3 %copy-start.9 = (f32[64,64]{1,0:T(8,128)}, f32[64,64]{1,0:T(8,128)S(1)}, u32[]{:S(2)}) copy-start(f32[64,64]{1,0:T(8,128)S(1)} %fusion.228) | copy-start | bytes 49156
  210.1 2.8 copy-start.2
  238.2 3.3 copy-start.6
  291.5 12.0 copy-start.7
  303.5 15.2 copy-start.10
  327.5 1.9 copy-start.5
  596.4 614.1 %reduce-scatter.5.cloned.1.call-start = ((), (), s32[]{:S(2)}) async-start(), calls=%async_computation.3 | async-start | bytes 270336 | tf_op jit(solution)/shard_map/reduce_scatter | solution.py:120
  804.2 1.9 copy-start.4
  1284.9 1.9 copy-start.3
  1537.0 5.7 copy-start.1
Sparse Core Ops, SparseCore 0:
  54.2 137.4 all-reduce.11
  596.5 133.2 reduce-scatter.2
  1077.6 132.8 reduce-scatter.4
where the time goes:
time: 1580 us; the launch traced here: 1550 us
  waiting for transfers between devices  403 us (26%)
  other arithmetic  392 us (25%)
  blocking collectives  249 us (16%)
  local copies, waits for them, and re-layouts  234 us (15%)
  between operations  155 us (10%)
  matrix products  115 us (7%)
    div x219, other arithmetic, lower_solve(): (target[column] - jnp.sum(factor[column] * result, axis=0)) / factor[colu...  267 us
    reduce_scatter x2, waiting for transfers between devices, per_device(): lax.psum_scatter(contract_rows(filled, ortho_rows), ('rows', 'sub'), scat...  266 us
    psum x1, waiting for transfers between devices, per_device(): gram_total, right_total = lax.psum((grams, right), ('rows', 'sub'))  137 us
    all_gather x2, blocking collectives, per_device(): mixer = lax.all_gather(mixer_share, ('rows', 'sub'), axis=0, tiled=True)  130 us
    psum x3, blocking collectives, per_device(): products = lax.psum(local_gram, ('rows', 'sub'))  119 us
    slice x192, local copies, waits for them, and re-layouts, cholesky_last(): diagonal_root = jnp.sqrt(remain[column])  113 us
    dot_general x3, matrix products, contract_rows(): lax.dot_general(former, latter, (((1,), (1,)), ((), ())), preferred_eleme...  42 us
    dot_general x4, matrix products, contract_first(): lax.dot_general(former, latter, (((0,), (0,)), ((), ())), preferred_eleme...  41.8 us
  transfers between devices with their start and end apart: 3, of which 3 were waited for; matrix products, arithmetic and copies ran while one was open for 0% of the time, Pallas kernels for 0%

commit v1 on v0

--- a/solution.py
+++ b/solution.py
@@ -113,7 +113,7 @@
             precision=highest,
             preferred_element_type=jnp.float32,
         )
-        products = lax.psum(local_gram, ("rows", "sub"))
+        products = lax.psum(lax.psum(local_gram, "sub"), "rows")
         inverse = inverse_factor(products)
         if sweep_index < POWER:
             ortho_rows = jnp.dot(inverse, sketch, precision=highest).astype(jnp.bfloat16)

time: 1580 us -> 1570 us (level)
    psum x3 -> x6, blocking collectives: 119 us -> 121 us  [per_device(): products = lax.psum(lax.psum(local_gram, 'sub'), 'rows')]
where the time goes in v1:
time: 1570 us; the launch traced here: 1550 us
  waiting for transfers between devices  399 us (25%)
  other arithmetic  392 us (25%)
  blocking collectives  250 us (16%)
  local copies, waits for them, and re-layouts  234 us (15%)
  between operations  155 us (10%)
  matrix products  115 us (7%)
    div x219, other arithmetic, lower_solve(): (target[column] - jnp.sum(factor[column] * result, axis=0)) / factor[colu...  267 us
    reduce_scatter x2, waiting for transfers between devices, per_device(): lax.psum_scatter(contract_rows(filled, ortho_rows), ('rows', 'sub'), scat...  262 us
    psum x1, waiting for transfers between devices, per_device(): gram_total, right_total = lax.psum((grams, right), ('rows', 'sub'))  137 us
    all_gather x2, blocking collectives, per_device(): mixer = lax.all_gather(mixer_share, ('rows', 'sub'), axis=0, tiled=True)  129 us
    psum x6, blocking collectives, per_device(): products = lax.psum(lax.psum(local_gram, 'sub'), 'rows')  121 us
    slice x192, local copies, waits for them, and re-layouts, cholesky_last(): diagonal_root = jnp.sqrt(remain[column])  113 us
    dot_general x3, matrix products, contract_rows(): lax.dot_general(former, latter, (((1,), (1,)), ((), ())), preferred_eleme...  42 us
    dot_general x4, matrix products, contract_first(): lax.dot_general(former, latter, (((0,), (0,)), ((), ())), preferred_eleme...  41.8 us
  transfers between devices with their start and end apart: 3, of which 3 were waited for; matrix products, arithmetic and copies ran while one was open for 0% of the time, Pallas kernels for 0%

profile of v1, /device:TPU:0, one launch (start us, length us, event | category | flops | bytes accessed | tf_op | source)
XLA Modules:
  0.0 1545.8 jit_solution(12233515524636403577)
XLA Ops:
  9.1 2.1 copy.518
  11.2 2.8 fusion.6
  14.1 2.5 copy.519
  16.6 12.9 mul.4308
  29.5 24.4 %fusion.2 = f32[32,512]{1,0:T(8,128)} fusion(bf16[32,16384]{1,0:T(8,128)(2,1)S(1)} %copy-done, bf16[512,16384]{1,0:T(8,128)(2,1)} %param.965, bf16[64,8,128,128]{3,2,1,0:T(8,128)(2,1)} %bitcast.3919), kind=kOutput, calls=%fused_computation.40 | convolution fusion | flops 545259520 | bytes 34668544 | tf_op jit(solution)/shard_map/dot_general | solution.py:78
  54.7 137.0 %all-reduce.12.cloned.1.call-done = (f32[32,32,512]{2,0,1:T(8,128)}, f32[32,512]{1,0:T(8,128)}) async-done(((f32[32,32,512]{2,0,1:T(8,128)}, f32[32,512]{1,0:T(8,128)}), (f32[32,32,512]{2,0,1:T(8,128)}, f32[32,512]{1,0:T(8,128)})) %all-reduce.12.cloned.1.call-update) | async-done | bytes 2162704 | tf_op jit(solution)/shard_map/psum | solution.py:100
  191.7 1.8 broadcast_add_fusion
  291.6 12.0 broadcast_in_dim.635
  303.6 15.2 bitcast_select_fusion
  318.8 8.8 fusion.224
  327.6 1.9 copy-done.5
  329.5 3.4 fusion.526
  332.9 18.1 %psum.58 = f32[64,64]{1,0:T(8,128)S(1)} all-reduce(f32[64,64]{1,0:T(8,128)S(1)} %fusion.526), channel_id=1, replica_groups=mesh['rows'=8,'sub'=4] {'sub'}, use_global_device_ids=true, to_apply=%region_97.98 | all-reduce | flops 4096 | bytes 32768 | tf_op jit(solution)/shard_map/psum | solution.py:116
  351.0 22.4 %psum.59 = f32[64,64,1]{1,0,2:T(8,128)S(1)} all-reduce(f32[64,64,1]{1,0,2:T(8,128)S(1)} %bitcast.3954), channel_id=1, replica_groups=mesh['rows'=8,'sub'=4] {'rows'}, use_global_device_ids=true, to_apply=%region_98.99 | all-reduce | flops 4096 | bytes 32768 | tf_op jit(solution)/shard_map/psum | solution.py:116
  501.0 1.4 fusion.504
  511.0 1.4 fusion.497
  516.8 1.4 fusion.493
  531.1 1.4 fusion.483
  538.3 1.4 fusion.478
  566.7 1.4 fusion.458
  579.5 1.4 fusion.449
  582.7 6.0 convolution_convert_fusion.2
  588.7 8.8 fusion.527
  597.6 130.8 %reduce-scatter.3.cloned.1.call-done = f32[16,64]{1,0:T(8,128)} async-done(((f32[512,64]{1,0:T(8,128)}), f32[16,64]{1,0:T(8,128)}) %reduce-scatter.3.cloned.1.call-update) | async-done | bytes 4112 | tf_op jit(solution)/shard_map/reduce_scatter | solution.py:120
  729.0 64.6 %all_gather.6 = bf16[512,64]{1,0:T(8,128)(2,1)S(1)} all-gather(bf16[16,64]{1,0:T(8,128)(2,1)S(1)} %convert_element_type.415), channel_id=1, replica_groups=mesh['rows'=8,'sub'=4] {'rows','sub'}, dimensions={0}, use_global_device_ids=true | all-gather | bytes 67584 | tf_op jit(solution)/shard_map/all_gather | solution.py:123
  793.6 8.9 fusion.528
  802.5 1.9 copy-done.4
  804.4 3.4 fusion.529
  807.8 17.8 %psum.60 = f32[64,64]{1,0:T(8,128)S(1)} all-reduce(f32[64,64]{1,0:T(8,128)S(1)} %fusion.529), channel_id=1, replica_groups=mesh['rows'=8,'sub'=4] {'sub'}, use_global_device_ids=true, to_apply=%region_227.228 | all-reduce | flops 4096 | bytes 32768 | tf_op jit(solution)/shard_map/psum | solution.py:116
  825.7 22.4 %psum.61 = f32[64,64,1]{1,0,2:T(8,128)S(1)} all-reduce(f32[64,64,1]{1,0,2:T(8,128)S(1)} %bitcast.3955), channel_id=1, replica_groups=mesh['rows'=8,'sub'=4] {'rows'}, use_global_device_ids=true, to_apply=%region_228.229 | all-reduce | flops 4096 | bytes 32768 | tf_op jit(solution)/shard_map/psum | solution.py:116
  968.8 1.9 subtract_divide_fusion.3
  970.8 1.4 fusion.447
  972.3 1.4 fusion.446
  978.0 1.4 fusion.442
  979.5 1.4 fusion.441
  989.5 1.4 fusion.434
  995.3 1.4 fusion.430
  1009.6 1.4 fusion.420
  1016.9 1.4 fusion.415
  1045.3 1.4 fusion.395
  1058.0 1.4 fusion.386
  1061.3 6.0 convolution_convert_fusion.1
  1067.2 8.8 fusion.530
  1076.1 130.8 %reduce-scatter.5.cloned.1.call-done = f32[16,64]{1,0:T(8,128)} async-done(((f32[512,64]{1,0:T(8,128)}), f32[16,64]{1,0:T(8,128)}) %reduce-scatter.5.cloned.1.call-update) | async-done | bytes 4112 | tf_op jit(solution)/shard_map/reduce_scatter | solution.py:120
  1207.5 64.7 %all_gather.7 = bf16[512,64]{1,0:T(8,128)(2,1)S(1)} all-gather(bf16[16,64]{1,0:T(8,128)(2,1)S(1)} %convert_element_type.417), channel_id=1, replica_groups=mesh['rows'=8,'sub'=4] {'rows','sub'}, dimensions={0}, use_global_device_ids=true | all-gather | bytes 67584 | tf_op jit(solution)/shard_map/all_gather | solution.py:123
  1272.2 8.9 fusion.531
  1281.1 1.9 copy-done.3
  1283.0 3.4 fusion.532
  1286.4 17.8 %psum.62 = f32[64,64]{1,0:T(8,128)S(1)} all-reduce(f32[64,64]{1,0:T(8,128)S(1)} %fusion.532), channel_id=1, replica_groups=mesh['rows'=8,'sub'=4] {'sub'}, use_global_device_ids=true, to_apply=%region_357.358 | all-reduce | flops 4096 | bytes 32768 | tf_op jit(solution)/shard_map/psum | solution.py:116
  1304.3 22.4 %psum.63 = f32[64,64,1]{1,0,2:T(8,128)S(1)} all-reduce(f32[64,64,1]{1,0,2:T(8,128)S(1)} %bitcast.3956), channel_id=1, replica_groups=mesh['rows'=8,'sub'=4] {'rows'}, use_global_device_ids=true, to_apply=%region_358.359 | all-reduce | flops 4096 | bytes 32768 | tf_op jit(solution)/shard_map/psum | solution.py:116
  1446.8 1.9 subtract_divide_fusion.2
  1448.8 1.4 fusion.384
  1451.7 1.4 fusion.382
  1459.0 1.4 fusion.377
  1463.3 1.4 fusion.374
  1464.7 1.4 fusion.373
  1467.6 1.4 fusion.371
  1479.0 1.4 fusion.363
  1494.8 1.4 fusion.352
  1504.9 1.4 fusion.345
  1516.3 1.4 fusion.337
  1526.3 1.4 fusion.330
  1529.1 1.4 fusion.328
  1533.3 5.7 convolution_multiply_fusion
  (2305 shorter events, 547.2 us)
Async XLA Ops:
  7.2 1.3 copy-start
  7.2 184.5 %all-reduce.12.cloned.1.call-start = ((), (), s32[]{:S(2)}) async-start(), calls=%async_computation.4 | async-start | bytes 4325376 | tf_op jit(solution)/shard_map/psum | solution.py:100
  9.1 2.1 copy-start.8
  54.0 674.3 %reduce-scatter.3.cloned.1.call-start = ((), (), s32[]{:S(2)}) async-start(), calls=%async_computation.2 | async-start | bytes 270336 | tf_op jit(solution)/shard_map/reduce_scatter | solution.py:120
  54.6 444.1 %copy-start.9 = (f32[64,64]{1,0:T(8,128)}, f32[64,64]{1,0:T(8,128)S(1)}, u32[]{:S(2)}) copy-start(f32[64,64]{1,0:T(8,128)S(1)} %fusion.228) | copy-start | bytes 49156
  210.2 2.8 copy-start.2
  238.2 3.3 copy-start.6
  291.6 12.0 copy-start.7
  303.6 15.2 copy-start.10
  327.5 1.9 copy-start.5
  597.5 609.3 %reduce-scatter.5.cloned.1.call-start = ((), (), s32[]{:S(2)}) async-start(), calls=%async_computation.3 | async-start | bytes 270336 | tf_op jit(solution)/shard_map/reduce_scatter | solution.py:120
  802.5 1.9 copy-start.4
  1281.1 1.9 copy-start.3
  1533.3 5.7 copy-start.1
Sparse Core Ops, SparseCore 0:
  54.1 137.5 all-reduce.11
  597.6 130.6 reduce-scatter.2
  1076.2 130.5 reduce-scatter.4
